TPU v7x, 128 devices: a whole 4x4x4 slice. The times are simulated.
128 devices in a mesh: attn: 8 (over x, core), ffn: 16 (over y, z).
Axes of the slice: x: 4, y: 4, z: 4, core: 2. Of those that a mesh axis runs over, the one named last changes fastest.
Arguments:
- queries: bfloat16 [1024, 2, 64, 576], P(('attn', 'ffn')), may hold values from -9 to 9
- latent_cache: bfloat16 [1024, 512, 576], P(('attn', 'ffn')), may hold values from -4 to 4
- fresh_latent: bfloat16 [1024, 2, 576], P(('attn', 'ffn')), may hold values from -4 to 4
- lengths: int32 [1024], P(('attn', 'ffn')), may hold values from 1 to 512, 262144 in all
- handoff: int32 [16, 8], P('ffn'), may hold values 0 or 1
- residual: bfloat16 [1024, 2, 7168], P(('attn', 'ffn')), may hold values from -30 to 30
- value_up_matrix: bfloat16 [64, 512, 128], P('ffn'), may hold values from -0.5 to 0.5
- output_weight: bfloat16 [8192, 7168], P('ffn'), may hold values from -0.1875 to 0.1875
- norm_gain: float32 [7168], replicated, may hold values from 0.3 to 3
- router: bfloat16 [7168, 16], replicated, may hold values from -0.0625 to 0.0625
- expert_ids: int32 [1024, 2, 2], P('attn'), may hold values from 0 to 15, all different within a row; in each aligned block of 256 rows (0 to 255, 256 to 511, ..., all dimensions but the last counted through in order) at most 64 rows name the same one
- gate_weight: bfloat16 [16, 7168, 2048], P('ffn', None, 'attn'), may hold values from -0.0625 to 0.0625
- up_weight: bfloat16 [16, 7168, 2048], P('ffn', None, 'attn'), may hold values from -0.0625 to 0.0625
- down_weight: bfloat16 [16, 2048, 7168], P('ffn', 'attn'), may hold values from -0.125 to 0.125
Outputs:
- attended: bfloat16 [1024, 2, 7168], P(('attn', 'ffn'))
- expert_out: bfloat16 [1024, 2, 7168], P(('attn', 'ffn'))
Inputs may be any that keep to these rules, and one draw needn't show every extreme that they name: `expert_ids`: the 2 ids of a token differ. In each aligned block of 256 tokens (the requests of one index of attn, all new tokens of each, in order) no expert is chosen by more than 64 tokens, and some expert is chosen by exactly 64 in some block.
All inputs are finite; a program needn't handle non-finite values. No bound on the sum of `lengths` or of `handoff` on one device may be relied on, other than what follows from the above.
Results may differ from a plain program's by a relative error of at most 0.014.
Values may be sent and summed in bfloat16 or wider, within the bound.
A program may use at most 128 MiB of HBM per device.

v0:
```python
import jax
import jax.numpy as jnp
from jax import lax
from jax.experimental import pallas as pl
from jax.experimental.pallas import tpu as pltpu
from jax.sharding import PartitionSpec as P

KV_RANK = 512


score_scale = 192.0 ** (-0.5)
norm_epsilon = 1e-06


MESH = pl.DeviceIdType.MESH
RING = 4
FLOWS = 8
F32 = jnp.float32
BF16 = jnp.bfloat16


class Wire:
    def __init__(self, send_sem, recv_sem):
        self.send_sem, self.recv_sem = send_sem, recv_sem
        self.copies, self.settled = [], []

    def send(self, src, dst, device):
        i = len(self.copies)
        copy = pltpu.make_async_remote_copy(
            src_ref=src,
            dst_ref=dst,
            send_sem=self.send_sem.at[i],
            recv_sem=self.recv_sem.at[i],
            device_id=device,
            device_id_type=MESH,
        )
        copy.start()
        self.copies.append(copy)
        return copy

    def settle(self, copies):
        for copy in copies:
            copy.wait_send()
            self.settled.append(copy)

    def drain(self):
        self.settle([c for c in self.copies if not any(c is d for d in self.settled)])


class Ring:
    def __init__(self, pos, device):
        self.pos, self.device = pos, device

    def index(self, by):
        return lax.rem(self.pos + by + RING, RING)

    def at(self, by):
        return self.device(self.index(by))


def rings():
    a, f = lax.axis_index("attn"), lax.axis_index("ffn")
    x, core = a // 2, lax.rem(a, 2)
    y, z = f // RING, lax.rem(f, RING)
    ring_x = Ring(x, lambda p: {"attn": p * 2 + core})
    ring_y = Ring(y, lambda p: {"ffn": p * RING + z})
    ring_z = Ring(z, lambda p: {"ffn": y * RING + p})
    return ring_x, ring_y, ring_z, core, {"attn": x * 2 + 1 - core}


def meet(devices):
    barrier = pltpu.get_barrier_semaphore()
    for device in devices:
        pl.semaphore_signal(barrier, inc=1, device_id=device, device_id_type=MESH)
    pl.semaphore_wait(barrier, len(devices))


class Scatter:
    def __init__(self, wire, ring, way, blocks, bufs, q):
        self.wire, self.ring, self.way, self.blocks = wire, ring, way, blocks
        self.relay, self.direct, self.final, self.stage = [b.at[q] for b in bufs]

    def start(self):
        r, s = self.ring, self.way
        self.c_relay = self.wire.send(self.blocks.at[r.index(2)], self.relay, r.at(s))
        self.c_direct = self.wire.send(self.blocks.at[r.index(-s)], self.direct, r.at(-s))

    def middle(self):
        r, s = self.ring, self.way
        self.c_relay.wait_recv()
        total = self.blocks[r.index(s)].astype(F32) + self.relay[...].astype(F32)
        self.stage[...] = total.astype(BF16)
        self.c_final = self.wire.send(self.stage, self.final, r.at(s))

    def finish(self):
        self.c_direct.wait_recv()
        self.c_final.wait_recv()
        return (
            self.blocks[self.ring.pos].astype(F32)
            + self.direct[...].astype(F32)
            + self.final[...].astype(F32)
        )

    def settle(self):
        self.wire.settle([self.c_relay, self.c_direct, self.c_final])


class Gather:
    def __init__(self, wire, ring, way, own, slot):
        self.wire, self.ring, self.way, self.own, self.slot = wire, ring, way, own, slot

    def start(self):
        r, s = self.ring, self.way
        here = self.slot(r.pos)
        self.c_on = self.wire.send(self.own, here, r.at(s))
        self.c_back = self.wire.send(self.own, here, r.at(-s))

    def middle(self):
        r, s = self.ring, self.way
        self.c_on.wait_recv()
        block = self.slot(r.index(-s))
        self.c_far = self.wire.send(block, block, r.at(s))

    def finish(self):
        self.c_back.wait_recv()
        self.c_far.wait_recv()


def way_of(q):
    return 1 if (q // 2) % 2 == 0 else -1


def waves(count, stages):
    for t in range(count + len(stages) - 1):
        for depth, stage in enumerate(stages):
            if 0 <= t - depth < count:
                stage(2 * (t - depth))
                stage(2 * (t - depth) + 1)


def slots_of(ids_ref, me_f, slots):
    half = ids_ref.shape[1]
    tokens = 2 * half
    ids = ids_ref[...].astype(F32).astype(BF16)
    request = lax.broadcasted_iota(jnp.int32, (half, tokens), 0)
    token = lax.broadcasted_iota(jnp.int32, (half, tokens), 1)
    spread = [
        jnp.dot(ids, (token == 2 * request + t).astype(F32).astype(BF16), preferred_element_type=F32)
        for t in range(2)
    ]
    named = [spread[0][k : k + 1] + spread[1][2 + k : 3 + k] for k in range(2)]
    mine = me_f.astype(F32)
    hit = jnp.where((named[0] == mine) | (named[1] == mine), 1.0, 0.0)
    row = lax.broadcasted_iota(jnp.int32, (tokens, tokens), 0)
    column = lax.broadcasted_iota(jnp.int32, (tokens, tokens), 1)
    before = (row <= column).astype(F32).astype(BF16)
    rank = jnp.dot(
        jnp.broadcast_to(hit, (8, tokens)).astype(BF16), before, preferred_element_type=F32
    )[0:1]
    slot = lax.broadcasted_iota(jnp.int32, (slots, tokens), 0).astype(F32)
    sel_yz = jnp.where((rank - 1.0 == slot) & (hit > 0.5), 1.0, 0.0).astype(BF16)
    source = (column % 64) // 16 * 64 + column // 64 * 16 + column % 16
    swap = (row == source).astype(F32).astype(BF16)
    sel_zy = jnp.dot(sel_yz, swap, preferred_element_type=F32).astype(BF16)
    expert = lax.broadcasted_iota(jnp.int32, (RING * RING, tokens), 0).astype(F32)
    chosen = jnp.where((named[0] == expert) | (named[1] == expert), 1.0, 0.0).astype(BF16)
    flags = lax.dot_general(
        sel_yz, chosen, (((1,), (1,)), ((), ())), preferred_element_type=F32
    )
    return sel_yz, sel_zy, flags


def layer_kernel(
    v_ref, wo_hbm, wg_hbm, wu_hbm, wd_hbm, res_ref, gain_ref, router_ref, ids_ref,
    attended_ref, out_ref,
    vt, wo, wgu, wd, state, normed, gathered, picked, selectors, rows_in, total, hidden,
    away, from_pair, px, p1, p2,
    x0, x1, x2, x3, a0, a1, a2, a3, b0, b1, b2, b3, send_sem, recv_sem, load_sem,
):
    ring_x, ring_y, ring_z, core, pair = rings()
    me_f = lax.axis_index("ffn")
    width = wo.shape[1] // FLOWS
    half = wd.shape[0]
    cols = [pl.ds(q * width, width) for q in range(FLOWS)]
    loads = []
    for q in range(FLOWS):
        load = pltpu.make_async_copy(wo_hbm.at[:, cols[q]], wo.at[:, cols[q]], load_sem.at[q])
        load.start()
        loads.append(load)
    late = [
        pltpu.make_async_copy(wg_hbm, wgu.at[:, pl.ds(0, half)], load_sem.at[FLOWS]),
        pltpu.make_async_copy(wu_hbm, wgu.at[:, pl.ds(half, half)], load_sem.at[FLOWS + 1]),
        pltpu.make_async_copy(wd_hbm, wd, load_sem.at[FLOWS + 2]),
    ]
    for load in late:
        load.start()
    for y in range(RING):
        for z in range(RING):
            vt[pl.ds((z * RING + y) * 16, 16), :] = v_ref[pl.ds((y * RING + z) * 16, 16), :]
    meet([ring_x.at(1), ring_x.at(-1), pair, ring_y.at(1), ring_y.at(-1), ring_z.at(1), ring_z.at(-1)])
    wire = Wire(send_sem, recv_sem)
    first = [ring_y if q % 2 == 0 else ring_z for q in range(FLOWS)]
    second = [ring_z if q % 2 == 0 else ring_y for q in range(FLOWS)]
    x_way = [1 if q % 2 == 0 else -1 for q in range(FLOWS)]

    def plane_scatter():
        return (
            [Scatter(wire, first[q], way_of(q), p1.at[q], (a0, a1, a2, a3), q) for q in range(FLOWS)],
            [Scatter(wire, second[q], way_of(q), p2.at[q], (b0, b1, b2, b3), q) for q in range(FLOWS)],
        )

    outer, inner = plane_scatter()
    squares = []

    def begin(q):
        loads[q].wait()
        rows = (v_ref if q % 2 == 0 else vt)[...]
        part = jnp.dot(rows, wo[:, cols[q]], preferred_element_type=F32)
        p1[q] = part.astype(BF16).reshape(RING, 64, width)
        outer[q].start()

    def turn(q):
        p2[q] = outer[q].finish().astype(BF16).reshape(RING, 16, width)
        inner[q].start()

    def close(q):
        own = inner[q].finish() + res_ref[:, cols[q]].astype(F32)
        state[q] = own
        attended_ref[:, cols[q]] = own.astype(BF16)
        squares.append(jnp.sum(own * own, axis=1, keepdims=True))

    waves(
        FLOWS // 2,
        [begin, lambda q: outer[q].middle(), turn, lambda q: inner[q].middle(), close],
    )
    scale = lax.rsqrt(sum(squares) / wo.shape[1] + norm_epsilon)

    small = [
        Gather(
            wire, first[q], way_of(q), normed.at[q],
            lambda p, q=q: gathered.at[q, second[q].pos, p],
        )
        for q in range(FLOWS)
    ]
    large = [
        Gather(
            wire, second[q], way_of(q), gathered.at[q, second[q].pos],
            lambda p, q=q: gathered.at[q, p],
        )
        for q in range(FLOWS)
    ]
    entry = [
        Gather(wire, ring_x, x_way[q], picked.at[q], lambda p, q=q: rows_in.at[q, core, p])
        for q in range(FLOWS)
    ]
    paired = [[] for _ in range(FLOWS)]
    logit_parts = []

    def share(q, by, src=None):
        block = rows_in.at[q, core, ring_x.index(by)]
        paired[q].append(wire.send(block if src is None else src, block, pair))

    def spread(q):
        value = (state[q] * scale * gain_ref[:, cols[q]]).astype(BF16)
        normed[q] = value
        gathered[q, second[q].pos, first[q].pos] = value
        small[q].start()

    def small_middle(q):
        small[q].middle()
        if q == 1:
            sel_yz, sel_zy, flags = slots_of(ids_ref, me_f, picked.shape[1])
            selectors[0] = sel_zy
            selectors[1] = sel_yz
            named.append(flags)

    named = []

    def widen(q):
        small[q].finish()
        large[q].start()

    def enter(q):
        large[q].finish()
        rows = gathered[q].reshape(RING * RING * 16, width)
        mine = jnp.dot(selectors[q % 2], rows, preferred_element_type=F32).astype(BF16)
        picked[q] = mine
        entry[q].start()
        share(q, 0, picked.at[q])
        rows_in[q, core, ring_x.pos] = mine
        logit_parts.append(
            lax.dot_general(
                mine, router_ref[:, cols[q]], (((1,), (1,)), ((), ())), preferred_element_type=F32
            )
        )

    def pass_on(q):
        entry[q].middle()
        share(q, -x_way[q])

    def arrive(q):
        entry[q].finish()
        share(q, x_way[q])
        share(q, 2)

    def absorb(q):
        for copy in paired[q]:
            copy.wait_recv()
        if q == 0:
            late[0].wait()
            late[1].wait()
        for c in range(2):
            block = rows_in[q, c].reshape(RING * picked.shape[1], width)
            part = jnp.dot(block, wgu[cols[q], :], preferred_element_type=F32)
            if q == 0:
                total[c] = part
            else:
                total[c] += part

    waves(
        FLOWS // 2,
        [
            spread, small_middle, widen, lambda q: large[q].middle(),
            enter, pass_on, arrive, absorb,
        ],
    )

    for c in range(2):
        gate, up = total[c, :, pl.ds(0, half)], total[c, :, pl.ds(half, half)]
        hidden[c] = (gate / (1.0 + jnp.exp(-gate)) * up).astype(BF16)
    late[2].wait()

    along = [Scatter(wire, ring_x, x_way[q], px.at[q], (x0, x1, x2, x3), q) for q in range(FLOWS)]
    outer_back, inner_back = plane_scatter()
    crossing = {}
    share_of = []

    def cross(q):
        part = jnp.dot(hidden[1 - core], wd[:, cols[q]], preferred_element_type=F32)
        away[q] = part.astype(BF16)
        crossing[q] = wire.send(away.at[q], from_pair.at[q], pair)

    def begin_back(q):
        part = jnp.dot(hidden[core], wd[:, cols[q]], preferred_element_type=F32)
        crossing[q].wait_recv()
        part = part + from_pair[q].astype(F32)
        px[q] = part.astype(BF16).reshape(RING, picked.shape[1], width)
        along[q].start()
        if q == 1:
            affinity = 1.0 / (1.0 + jnp.exp(-sum(logit_parts)))
            column = lax.broadcasted_iota(jnp.int32, affinity.shape, 1)
            mine = jnp.sum(jnp.where(column == me_f, affinity, 0.0), axis=1, keepdims=True)
            both = jnp.sum(affinity * named[0], axis=1, keepdims=True)
            share_of.append(2.5 * mine / jnp.where(both > 0.0, both, 1.0))

    def combine(q):
        outer[q].settle()
        inner[q].settle()
        rows = along[q].finish().astype(BF16).astype(F32)
        rows = (rows * share_of[0]).astype(BF16)
        back = lax.dot_general(
            selectors[1 - q % 2], rows, (((0,), (0,)), ((), ())), preferred_element_type=F32
        )
        p1[q] = back.astype(BF16).reshape(RING, 64, width)
        outer_back[q].start()

    def turn_back(q):
        p2[q] = outer_back[q].finish().astype(BF16).reshape(RING, 16, width)
        inner_back[q].start()

    def close_back(q):
        out_ref[:, cols[q]] = inner_back[q].finish().astype(BF16)

    waves(
        FLOWS // 2,
        [
            cross, begin_back, lambda q: along[q].middle(), combine,
            lambda q: outer_back[q].middle(), turn_back,
            lambda q: inner_back[q].middle(), close_back,
        ],
    )
    wire.drain()


def vmem_specs(count):
    return [pl.BlockSpec(memory_space=pltpu.VMEM)] * count


def exchange_bufs(rows, width):
    return [pltpu.VMEM((FLOWS, rows, width), BF16)] * 4


PIECE = 16
VMEM_LIMIT = 66 * 1024 * 1000
SENDS = 2


def attend_kernel(
    len_ref, hand_ref, q_hbm, kt_hbm, fresh_ref, w_ref,
    v_ref,
    flag_ref, q, kt, sent, got, flags, values, passed, send_sem, recv_sem, load_sem,
):
    _, ring_y, ring_z, _, _ = rings()
    a, f = lax.axis_index("attn"), lax.axis_index("ffn")
    count = lax.axis_size("attn")
    onward = {"attn": lax.rem(a + 1, count)}
    behind = {"attn": lax.rem(a + count - 1, count)}
    requests, rows, rank = q.shape[0], q.shape[1], w_ref.shape[1]
    heads = rows // 2
    loads = []
    for r in range(requests):
        pair = (
            pltpu.make_async_copy(q_hbm.at[r], q.at[r], load_sem.at[2 * r]),
            pltpu.make_async_copy(kt_hbm.at[r], kt.at[r], load_sem.at[2 * r + 1]),
        )
        for load in pair:
            load.start()
        loads.append(pair)
    offsets = [(dy, dz) for dy in (2, 1, 3, 0) for dz in (2, 1, 3, 0) if (dy, dz) != (0, 0)]

    def peer(dy, dz):
        return ring_y.index(dy) * RING + ring_z.index(dz)

    token = lax.broadcasted_iota(jnp.int32, flag_ref.shape, 0) // 2
    flag = jnp.zeros(flag_ref.shape, F32)
    for r in range(requests):
        flag = jnp.where(token == r, hand_ref[0, r].astype(F32), flag)
    flag_ref[...] = flag.astype(BF16)
    flags[ring_y.pos, ring_z.pos] = flag.astype(BF16)
    meet([{"ffn": peer(dy, dz)} for dy, dz in offsets] + [onward, behind])
    wire = Wire(send_sem, recv_sem)
    flag_copies = {}
    for dy, dz in offsets:
        flag_copies[dy, dz] = wire.send(
            flag_ref, flags.at[ring_y.pos, ring_z.pos], {"ffn": peer(dy, dz)}
        )

    place = lax.broadcasted_iota(jnp.int32, (2 * rows, 2 * rows), 0)
    source = lax.broadcasted_iota(jnp.int32, (2 * rows, 2 * rows), 1)
    wanted = (
        (place % 16) // 8 * rows + (place % 8) // 4 * heads + place // 16 * 4 + place % 4
    )
    order = (source == wanted).astype(F32).astype(BF16)
    position = lax.broadcasted_iota(jnp.int32, (rows, kt.shape[2]), 1)
    step = lax.broadcasted_iota(jnp.int32, (rows, fresh_ref.shape[1]), 0) // heads
    column = lax.broadcasted_iota(jnp.int32, (rows, fresh_ref.shape[1]), 1)
    across = (((1,), (1,)), ((), ()))

    def attend(r):
        for load in loads[r]:
            load.wait()
        old = jnp.dot(q[r], kt[r], preferred_element_type=F32) * score_scale
        old = jnp.where(position < len_ref[r], old, -jnp.inf)
        new = lax.dot_general(q[r], fresh_ref[r], across, preferred_element_type=F32) * score_scale
        new = jnp.where(column <= step, new, -jnp.inf)
        peak = jnp.maximum(
            jnp.max(old, axis=1, keepdims=True), jnp.max(new, axis=1, keepdims=True)
        )
        old, new = jnp.exp(old - peak), jnp.exp(new - peak)
        below = jnp.sum(old, axis=1, keepdims=True) + jnp.sum(new, axis=1, keepdims=True)
        mixed = lax.dot_general(
            (old / below).astype(BF16), kt[r, pl.ds(0, rank), :], across, preferred_element_type=F32
        )
        mixed = mixed + jnp.dot(
            (new / below).astype(BF16), fresh_ref[r, :, pl.ds(0, rank)], preferred_element_type=F32
        )
        return mixed.astype(BF16)

    pairs = requests // 2
    per_send = pairs // SENDS
    copies = {}
    for p in range(pairs):
        both = jnp.concatenate([attend(2 * p), attend(2 * p + 1)], axis=0)
        piece = jnp.dot(order, both, preferred_element_type=F32).astype(BF16)
        sent[:, p] = piece.reshape(RING * RING, PIECE, rank)
        if (p + 1) % per_send == 0:
            part = pl.ds(p + 1 - per_send, per_send)
            for dy, dz in offsets:
                to = peer(dy, dz)
                copies.setdefault(dy, []).append(
                    wire.send(sent.at[to, part], got.at[ring_y.pos, ring_z.pos, part], {"ffn": to})
                )
    got[ring_y.pos, ring_z.pos] = sent[f]

    block_rows = RING * pairs * PIECE
    tokens = block_rows // 4
    gather = (
        lax.broadcasted_iota(jnp.int32, (tokens, block_rows), 1) // 4
        == lax.broadcasted_iota(jnp.int32, (tokens, block_rows), 0)
    ).astype(F32).astype(BF16)
    head = lax.broadcasted_iota(jnp.int32, (block_rows, w_ref.shape[2]), 0) % 4
    shifts = {}
    turns = (0, 1, 3, 2)
    for dy in turns:
        for copy in copies[dy]:
            copy.wait_recv()
        block = ring_y.index(-dy)
        latents = got[block].reshape(block_rows, rank)
        mapped = [
            jnp.where(
                head == j, jnp.dot(latents, w_ref[j], preferred_element_type=F32), 0.0
            ).astype(BF16)
            for j in range(w_ref.shape[0])
        ]
        value = jnp.dot(gather, jnp.concatenate(mapped, axis=1), preferred_element_type=F32)
        values[block] = value.astype(BF16)
        shifts[dy] = wire.send(values.at[block], passed.at[block], onward)
    for dy, dz in offsets:
        flag_copies[dy, dz].wait_recv()
    for dy in turns:
        shifts[dy].wait_recv()
        block = ring_y.index(-dy)
        flag = flags[block].reshape(tokens, flag_ref.shape[1]).astype(F32)
        moved = jnp.concatenate([flag] * (values.shape[2] // flag.shape[1]), axis=1) > 0.5
        v_ref[block] = jnp.where(moved, passed[block].astype(F32), values[block].astype(F32)).astype(BF16)
    wire.drain()


def attend(queries, cache, fresh, lengths, handoff, value_up):
    requests, steps, heads, latent = queries.shape
    span = cache.shape[1]
    per_dev, rank, v_head = value_up.shape
    rows = steps * heads
    plane = RING * RING
    copies = (plane - 1) * (1 + SENDS) + RING
    tokens = RING * requests * steps
    return pl.pallas_call(
        attend_kernel,
        name="attend",
        out_shape=jax.ShapeDtypeStruct((RING, tokens, per_dev * v_head), BF16),
        in_specs=[pl.BlockSpec(memory_space=pltpu.SMEM)] * 2
        + [pl.BlockSpec(memory_space=pl.ANY)] * 2
        + vmem_specs(2),
        out_specs=vmem_specs(1)[0],
        scratch_shapes=[
            pltpu.VMEM((requests * steps, 128), BF16),
            pltpu.VMEM((requests, rows, latent), BF16),
            pltpu.VMEM((requests, latent, span), BF16),
            pltpu.VMEM((plane, requests // 2, PIECE, rank), BF16),
            pltpu.VMEM((RING, RING, requests // 2, PIECE, rank), BF16),
            pltpu.VMEM((RING, RING, requests * steps, 128), BF16),
            pltpu.VMEM((RING, tokens, per_dev * v_head), BF16),
            pltpu.VMEM((RING, tokens, per_dev * v_head), BF16),
            pltpu.SemaphoreType.DMA((copies,)),
            pltpu.SemaphoreType.DMA((copies,)),
            pltpu.SemaphoreType.DMA((2 * requests,)),
        ],
        compiler_params=pltpu.CompilerParams(collective_id=3, has_side_effects=True),
    )(
        lengths,
        handoff,
        queries.reshape(requests, rows, latent),
        jnp.swapaxes(cache, 1, 2),
        fresh,
        value_up,
    )


def layer(v, output_weight, gate, up, down, residual, norm_gain, router_t, ids):
    depth, model_width = output_weight.shape
    width = model_width // FLOWS
    half = down.shape[0]
    tokens, slots = v.shape[0], 4 * residual.shape[0]
    copies = (12 + 7 + 1 + 9) * FLOWS
    return pl.pallas_call(
        layer_kernel,
        name="layer",
        out_shape=(
            jax.ShapeDtypeStruct((tokens // 16, model_width), BF16),
            jax.ShapeDtypeStruct((tokens // 16, model_width), BF16),
        ),
        in_specs=vmem_specs(1) + [pl.BlockSpec(memory_space=pl.ANY)] * 4 + vmem_specs(4),
        out_specs=tuple(vmem_specs(2)),
        scratch_shapes=[
            pltpu.VMEM((tokens, depth), BF16),
            pltpu.VMEM((depth, model_width), BF16),
            pltpu.VMEM((model_width, 2 * half), BF16),
            pltpu.VMEM((half, model_width), BF16),
            pltpu.VMEM((FLOWS, 16, width), F32),
            pltpu.VMEM((FLOWS, 16, width), BF16),
            pltpu.VMEM((FLOWS, RING, RING, 16, width), BF16),
            pltpu.VMEM((FLOWS, slots, width), BF16),
            pltpu.VMEM((2, slots, tokens), BF16),
            pltpu.VMEM((FLOWS, 2, RING, slots, width), BF16),
            pltpu.VMEM((2, RING * slots, 2 * half), F32),
            pltpu.VMEM((2, RING * slots, half), BF16),
            pltpu.VMEM((FLOWS, RING * slots, width), BF16),
            pltpu.VMEM((FLOWS, RING * slots, width), BF16),
            pltpu.VMEM((FLOWS, RING, slots, width), BF16),
            pltpu.VMEM((FLOWS, RING, 64, width), BF16),
            pltpu.VMEM((FLOWS, RING, 16, width), BF16),
            *exchange_bufs(slots, width),
            *exchange_bufs(64, width),
            *exchange_bufs(16, width),
            pltpu.SemaphoreType.DMA((copies,)),
            pltpu.SemaphoreType.DMA((copies,)),
            pltpu.SemaphoreType.DMA((FLOWS + 3,)),
        ],
        compiler_params=pltpu.CompilerParams(
            collective_id=1, has_side_effects=True, vmem_limit_bytes=VMEM_LIMIT
        ),
    )(v, output_weight, gate, up, down, residual, norm_gain, router_t, ids)


def local(
    queries,
    latent_cache,
    fresh_latent,
    lengths,
    handoff,
    residual,
    value_up_matrix,
    output_weight,
    norm_gain,
    router,
    expert_ids,
    gate_weight,
    up_weight,
    down_weight,
):
    heads_local, _, v_head = value_up_matrix.shape
    req_dev, steps_here, model_width = residual.shape
    row_tokens = expert_ids.shape[0] * steps_here
    value_rows = attend(queries, latent_cache, fresh_latent, lengths, handoff, value_up_matrix)
    attended, summed = layer(
        value_rows.reshape(row_tokens, heads_local * v_head),
        output_weight,
        gate_weight[0],
        up_weight[0],
        down_weight[0],
        residual.reshape(req_dev * steps_here, model_width),
        norm_gain.reshape(1, model_width),
        router.T,
        jnp.transpose(expert_ids, (1, 2, 0)).reshape(-1, expert_ids.shape[0]),
    )
    return (attended.reshape(residual.shape), summed.reshape(residual.shape))


def solution(mesh):
    return jax.shard_map(
        local,
        mesh=mesh,
        in_specs=(
            P(("attn", "ffn"), None, None, None),
            P(("attn", "ffn"), None, None),
            P(("attn", "ffn"), None, None),
            P(("attn", "ffn")),
            P("ffn", None),
            P(("attn", "ffn"), None, None),
            P("ffn", None, None),
            P("ffn", None),
            P(),
            P(),
            P("attn", None, None),
            P("ffn", None, "attn"),
            P("ffn", None, "attn"),
            P("ffn", "attn", None),
        ),
        out_specs=(P(("attn", "ffn"), None, None), P(("attn", "ffn"), None, None)),
        check_vma=False,
    )
```

profile of v0, /device:TPU:0, one launch (start us, length us, event | category | flops | bytes accessed | tf_op | source)
XLA Modules:
  0.0 172.4 jit_solution(9091410329285983813)
XLA Ops:
  0.6 1.7 reshape.27.res_ref
  2.3 32.8 %attend.1 = bf16[4,64,512]{2,1,0:T(8,128)(2,1)} custom-call(s32[8]{0:T(128)} %len_ref.1, s32[1,8]{1,0:T(1,128)} %hand_ref.1, bf16[8,128,576]{2,1,0:T(8,128)(2,1)} %bitcast.15, bf16[8,576,512]{2,1,0:T(8,128)(2,1)} %bitcast.11, bf16[8,2,576]{2,1,0:T(2,128)(2,1)} %fresh_ref.1, bf16[4,512,128]{2,1,0:T(8,128)(2,1)} %w_ref.1), custom_call_target="tpu_custom_call" | custom-call | tf_op jit(solution)/shard_map/attend/pallas_call | solution.py:527
  35.2 133.8 %layer.1 = (bf16[16,7168]{1,0:T(8,128)(2,1)}, bf16[16,7168]{1,0:T(8,128)(2,1)}) custom-call(bf16[256,512]{1,0:T(8,128)(2,1)} %bitcast.16, bf16[512,7168]{1,0:T(8,128)(2,1)} %wo_hbm.1, bf16[7168,256]{1,0:T(8,128)(2,1)} %bitcast.12, bf16[7168,256]{1,0:T(8,128)(2,1)} %bitcast.13, bf16[256,7168]{1,0:T(8,128)(2,1)} %bitcast.14, ...), custom_call_target="tpu_custom_call" | custom-call | tf_op jit(solution)/shard_map/layer/pallas_call | solution.py:565
  169.0 1.7 reshape.30
  170.7 1.7 reshape.31
where the time goes:
time: 173 us; the launch traced here: 172 us
  Pallas kernels  167 us (97%)
  local copies, waits for them, and re-layouts  5.14 us (3%)
    pallas_call x1, Pallas kernels, layer(): pl.pallas_call(layer_kernel, name='layer', out_shape=(jax.ShapeDtypeStruc...  134 us
    pallas_call x1, Pallas kernels, attend(): pl.pallas_call(attend_kernel, name='attend', out_shape=jax.ShapeDtypeStru...  32.8 us

commit v1 on v0

--- a/solution.py
+++ b/solution.py
@@ -14,7 +14,7 @@
 
 MESH = pl.DeviceIdType.MESH
 RING = 4
-FLOWS = 8
+FLOWS = 14
 F32 = jnp.float32
 BF16 = jnp.bfloat16
 
@@ -126,14 +126,32 @@
         self.c_far.wait_recv()
 
 
-def way_of(q):
-    return 1 if (q // 2) % 2 == 0 else -1
+class Trade:
+    def __init__(self, wire, ring, source, target):
+        self.wire, self.ring, self.source, self.target = wire, ring, source, target
+
+    def start(self):
+        self.copies = [
+            self.wire.send(self.source(self.ring.index(k)), self.target(k), self.ring.at(k))
+            for k in (2, 1, 3)
+        ]
+
+    def finish(self):
+        for copy in self.copies:
+            copy.wait_recv()
+
+    def settle(self):
+        self.wire.settle(self.copies)
+
+
+def way_of(q, core):
+    return (1 if (q // 2) % 2 == 0 else -1) * (1 - 2 * core)
 
 
 def waves(count, stages):
     for t in range(count + len(stages) - 1):
         for depth, stage in enumerate(stages):
-            if 0 <= t - depth < count:
+            if stage is not None and 0 <= t - depth < count:
                 stage(2 * (t - depth))
                 stage(2 * (t - depth) + 1)
 
@@ -173,12 +191,13 @@
 def layer_kernel(
     v_ref, wo_hbm, wg_hbm, wu_hbm, wd_hbm, res_ref, gain_ref, router_ref, ids_ref,
     attended_ref, out_ref,
-    vt, wo, wgu, wd, state, normed, gathered, picked, selectors, rows_in, total, hidden,
+    vt, wo, wgu, wd, normed, scales, gathered, picked, selectors, slot_scales, rows_in, total, hidden,
     away, from_pair, px, p1, p2,
-    x0, x1, x2, x3, a0, a1, a2, a3, b0, b1, b2, b3, send_sem, recv_sem, load_sem,
+    x0, x1, x2, x3, a0, a1, a2, a3, b1, b2, b3, send_sem, recv_sem, load_sem,
 ):
     ring_x, ring_y, ring_z, core, pair = rings()
-    me_f = lax.axis_index("ffn")
+    a, me_f = lax.axis_index("attn"), lax.axis_index("ffn")
+    count = lax.axis_size("attn")
     width = wo.shape[1] // FLOWS
     half = wd.shape[0]
     cols = [pl.ds(q * width, width) for q in range(FLOWS)]
@@ -197,7 +216,14 @@
     for y in range(RING):
         for z in range(RING):
             vt[pl.ds((z * RING + y) * 16, 16), :] = v_ref[pl.ds((y * RING + z) * 16, 16), :]
-    meet([ring_x.at(1), ring_x.at(-1), pair, ring_y.at(1), ring_y.at(-1), ring_z.at(1), ring_z.at(-1)])
+    column_peers = [{"attn": lax.rem(a + k, count)} for k in range(1, count)]
+    plane_peers = [
+        {"ffn": ring_y.index(dy) * RING + ring_z.index(dz)}
+        for dy in range(RING)
+        for dz in range(RING)
+        if (dy, dz) != (0, 0)
+    ]
+    meet(column_peers + plane_peers)
     wire = Wire(send_sem, recv_sem)
     first = [ring_y if q % 2 == 0 else ring_z for q in range(FLOWS)]
     second = [ring_z if q % 2 == 0 else ring_y for q in range(FLOWS)]
@@ -205,12 +231,24 @@
 
     def plane_scatter():
         return (
-            [Scatter(wire, first[q], way_of(q), p1.at[q], (a0, a1, a2, a3), q) for q in range(FLOWS)],
-            [Scatter(wire, second[q], way_of(q), p2.at[q], (b0, b1, b2, b3), q) for q in range(FLOWS)],
-        )
+            [Scatter(wire, first[q], way_of(q, core), p1.at[q], (a0, a1, a2, a3), q) for q in range(FLOWS)],
+            [
+                Trade(
+                    wire, second[q],
+                    lambda p, q=q: p2.at[q, p],
+                    lambda k, q=q: (b1, b2, b3)[k - 1].at[q],
+                )
+                for q in range(FLOWS)
+            ],
+        )
+
+    def inner_sum(q, trade):
+        trade.finish()
+        own = p2[q, second[q].pos].astype(F32)
+        return own + b1[q].astype(F32) + b2[q].astype(F32) + b3[q].astype(F32)
 
     outer, inner = plane_scatter()
-    squares = []
+    squares, named, own_scale = [], [], []
 
     def begin(q):
         loads[q].wait()
@@ -222,29 +260,55 @@
     def turn(q):
         p2[q] = outer[q].finish().astype(BF16).reshape(RING, 16, width)
         inner[q].start()
+        if q == 1:
+            sel_yz, sel_zy, flags = slots_of(ids_ref, me_f, picked.shape[1])
+            selectors[0] = sel_zy
+            selectors[1] = sel_yz
+            named.append(flags)
+
+    scale_copies, slot_copies = [], []
 
     def close(q):
-        own = inner[q].finish() + res_ref[:, cols[q]].astype(F32)
-        state[q] = own
+        own = inner_sum(q, inner[q]) + res_ref[:, cols[q]].astype(F32)
         attended_ref[:, cols[q]] = own.astype(BF16)
         squares.append(jnp.sum(own * own, axis=1, keepdims=True))
-
-    waves(
-        FLOWS // 2,
-        [begin, lambda q: outer[q].middle(), turn, lambda q: inner[q].middle(), close],
-    )
-    scale = lax.rsqrt(sum(squares) / wo.shape[1] + norm_epsilon)
+        value = (own * gain_ref[:, cols[q]]).astype(BF16)
+        normed[q] = value
+        gathered[q, second[q].pos, first[q].pos] = value
+        small[q].start()
+        if q == FLOWS - 1:
+            scale = lax.rsqrt(sum(squares) / wo.shape[1] + norm_epsilon)
+            here = scales.at[ring_y.pos, ring_z.pos]
+            here[...] = jnp.broadcast_to(scale, here.shape)
+            for peer in plane_peers:
+                scale_copies.append(wire.send(here, here, peer))
+
+    def scale_slots():
+        for copy in scale_copies:
+            copy.wait_recv()
+        rest = scales[...].reshape(RING * RING * 16, scales.shape[3])
+        found = jnp.zeros((picked.shape[1], scales.shape[3]), F32)
+        for _ in range(3):
+            part = rest.astype(BF16)
+            found += jnp.dot(selectors[1], part, preferred_element_type=F32)
+            rest = rest - part.astype(F32)
+        here = slot_scales.at[core, ring_x.pos]
+        here[...] = found
+        for peer in column_peers:
+            slot_copies.append(wire.send(here, here, peer))
+        return found
 
     small = [
-        Gather(
-            wire, first[q], way_of(q), normed.at[q],
-            lambda p, q=q: gathered.at[q, second[q].pos, p],
+        Trade(
+            wire, first[q],
+            lambda p, q=q: normed.at[q],
+            lambda k, q=q: gathered.at[q, second[q].pos, first[q].pos],
         )
         for q in range(FLOWS)
     ]
     large = [
         Gather(
-            wire, second[q], way_of(q), gathered.at[q, second[q].pos],
+            wire, second[q], way_of(q, core), gathered.at[q, second[q].pos],
             lambda p, q=q: gathered.at[q, p],
         )
         for q in range(FLOWS)
@@ -260,21 +324,6 @@
         block = rows_in.at[q, core, ring_x.index(by)]
         paired[q].append(wire.send(block if src is None else src, block, pair))
 
-    def spread(q):
-        value = (state[q] * scale * gain_ref[:, cols[q]]).astype(BF16)
-        normed[q] = value
-        gathered[q, second[q].pos, first[q].pos] = value
-        small[q].start()
-
-    def small_middle(q):
-        small[q].middle()
-        if q == 1:
-            sel_yz, sel_zy, flags = slots_of(ids_ref, me_f, picked.shape[1])
-            selectors[0] = sel_zy
-            selectors[1] = sel_yz
-            named.append(flags)
-
-    named = []
 
     def widen(q):
         small[q].finish()
@@ -304,6 +353,8 @@
         share(q, 2)
 
     def absorb(q):
+        if q == 1:
+            own_scale.append(scale_slots())
         for copy in paired[q]:
             copy.wait_recv()
         if q == 0:
@@ -320,13 +371,18 @@
     waves(
         FLOWS // 2,
         [
-            spread, small_middle, widen, lambda q: large[q].middle(),
-            enter, pass_on, arrive, absorb,
+            begin, lambda q: outer[q].middle(), turn, close, widen,
+            lambda q: large[q].middle(), enter, pass_on, arrive, absorb,
         ],
     )
 
+    for copy in slot_copies:
+        copy.wait_recv()
     for c in range(2):
-        gate, up = total[c, :, pl.ds(0, half)], total[c, :, pl.ds(half, half)]
+        scale = slot_scales[c].reshape(RING * picked.shape[1], slot_scales.shape[3])
+        scale = jnp.concatenate([scale] * (half // scale.shape[1]), axis=1)
+        gate = total[c, :, pl.ds(0, half)] * scale
+        up = total[c, :, pl.ds(half, half)] * scale
         hidden[c] = (gate / (1.0 + jnp.exp(-gate)) * up).astype(BF16)
     late[2].wait()
 
@@ -347,7 +403,8 @@
         px[q] = part.astype(BF16).reshape(RING, picked.shape[1], width)
         along[q].start()
         if q == 1:
-            affinity = 1.0 / (1.0 + jnp.exp(-sum(logit_parts)))
+            logits = sum(logit_parts) * own_scale[0][:, : router_ref.shape[0]]
+            affinity = 1.0 / (1.0 + jnp.exp(-logits))
             column = lax.broadcasted_iota(jnp.int32, affinity.shape, 1)
             mine = jnp.sum(jnp.where(column == me_f, affinity, 0.0), axis=1, keepdims=True)
             both = jnp.sum(affinity * named[0], axis=1, keepdims=True)
@@ -369,14 +426,13 @@
         inner_back[q].start()
 
     def close_back(q):
-        out_ref[:, cols[q]] = inner_back[q].finish().astype(BF16)
+        out_ref[:, cols[q]] = inner_sum(q, inner_back[q]).astype(BF16)
 
     waves(
         FLOWS // 2,
         [
             cross, begin_back, lambda q: along[q].middle(), combine,
-            lambda q: outer_back[q].middle(), turn_back,
-            lambda q: inner_back[q].middle(), close_back,
+            lambda q: outer_back[q].middle(), turn_back, close_back,
         ],
     )
     wire.drain()
@@ -561,7 +617,7 @@
     width = model_width // FLOWS
     half = down.shape[0]
     tokens, slots = v.shape[0], 4 * residual.shape[0]
-    copies = (12 + 7 + 1 + 9) * FLOWS
+    copies = (12 + 7 + 1 + 9) * FLOWS + 15 + 7
     return pl.pallas_call(
         layer_kernel,
         name="layer",
@@ -576,11 +632,12 @@
             pltpu.VMEM((depth, model_width), BF16),
             pltpu.VMEM((model_width, 2 * half), BF16),
             pltpu.VMEM((half, model_width), BF16),
-            pltpu.VMEM((FLOWS, 16, width), F32),
             pltpu.VMEM((FLOWS, 16, width), BF16),
+            pltpu.VMEM((RING, RING, 16, 128), F32),
             pltpu.VMEM((FLOWS, RING, RING, 16, width), BF16),
             pltpu.VMEM((FLOWS, slots, width), BF16),
             pltpu.VMEM((2, slots, tokens), BF16),
+            pltpu.VMEM((2, RING, slots, 128), F32),
             pltpu.VMEM((FLOWS, 2, RING, slots, width), BF16),
             pltpu.VMEM((2, RING * slots, 2 * half), F32),
             pltpu.VMEM((2, RING * slots, half), BF16),
@@ -591,7 +648,7 @@
             pltpu.VMEM((FLOWS, RING, 16, width), BF16),
             *exchange_bufs(slots, width),
             *exchange_bufs(64, width),
-            *exchange_bufs(16, width),
+            *exchange_bufs(16, width)[1:],
             pltpu.SemaphoreType.DMA((copies,)),
             pltpu.SemaphoreType.DMA((copies,)),
             pltpu.SemaphoreType.DMA((FLOWS + 3,)),

time: 173 us -> 168 us (0.971)
  Pallas kernels: 167 us -> 162 us
    pallas_call x1, Pallas kernels: 134 us -> 129 us  [layer(): pl.pallas_call(layer_kernel, name='layer', out_shape=(jax.ShapeDtypeStruc...]
where the time goes in v1:
time: 168 us; the launch traced here: 167 us
  Pallas kernels  162 us (96%)
  local copies, waits for them, and re-layouts  5.14 us (3%)
    pallas_call x1, Pallas kernels, layer(): pl.pallas_call(layer_kernel, name='layer', out_shape=(jax.ShapeDtypeStruc...  129 us
    pallas_call x1, Pallas kernels, attend(): pl.pallas_call(attend_kernel, name='attend', out_shape=jax.ShapeDtypeStru...  32.8 us
    reshape x2, local copies, waits for them, and re-layouts, local(): return (attended.reshape(residual.shape), summed.reshape(residual.shape))  3.42 us

profile of v1, /device:TPU:0, one launch (start us, length us, event | category | flops | bytes accessed | tf_op | source)
XLA Modules:
  0.0 167.4 jit_solution(8372183960543853352)
XLA Ops:
  0.6 1.7 %reshape.27.res_ref = bf16[16,7168]{1,0:T(8,128)(2,1)} reshape(bf16[8,2,7168]{2,1,0:T(2,128)(2,1)} %param.19) | data formatting | bytes 458752 | tf_op jit(solution)/shard_map/reshape | solution.py:688
  2.3 32.8 %attend.1 = bf16[4,64,512]{2,1,0:T(8,128)(2,1)} custom-call(s32[8]{0:T(128)} %len_ref.1, s32[1,8]{1,0:T(1,128)} %hand_ref.1, bf16[8,128,576]{2,1,0:T(8,128)(2,1)} %bitcast.15, bf16[8,576,512]{2,1,0:T(8,128)(2,1)} %bitcast.11, bf16[8,2,576]{2,1,0:T(2,128)(2,1)} %fresh_ref.1, bf16[4,512,128]{2,1,0:T(8,128)(2,1)} %w_ref.1), custom_call_target="tpu_custom_call" | custom-call | tf_op jit(solution)/shard_map/attend/pallas_call | solution.py:583
  35.2 128.8 %layer.1 = (bf16[16,7168]{1,0:T(8,128)(2,1)}, bf16[16,7168]{1,0:T(8,128)(2,1)}) custom-call(bf16[256,512]{1,0:T(8,128)(2,1)} %bitcast.16, bf16[512,7168]{1,0:T(8,128)(2,1)} %wo_hbm.1, bf16[7168,256]{1,0:T(8,128)(2,1)} %bitcast.12, bf16[7168,256]{1,0:T(8,128)(2,1)} %bitcast.13, bf16[256,7168]{1,0:T(8,128)(2,1)} %bitcast.14, ...), custom_call_target="tpu_custom_call" | custom-call | tf_op jit(solution)/shard_map/layer/pallas_call | solution.py:621
  164.0 1.7 %reshape.30 = bf16[8,2,7168]{2,1,0:T(2,128)(2,1)} reshape(bf16[16,7168]{1,0:T(8,128)(2,1)} %get-tuple-element.4) | data formatting | bytes 458752 | tf_op jit(solution)/shard_map/reshape | solution.py:693
  165.7 1.7 %reshape.31 = bf16[8,2,7168]{2,1,0:T(2,128)(2,1)} reshape(bf16[16,7168]{1,0:T(8,128)(2,1)} %get-tuple-element.5) | data formatting | bytes 458752 | tf_op jit(solution)/shard_map/reshape | solution.py:693

commit v2 on v1

--- a/solution.py
+++ b/solution.py
@@ -269,8 +269,8 @@
     scale_copies, slot_copies = [], []
 
     def close(q):
-        own = inner_sum(q, inner[q]) + res_ref[:, cols[q]].astype(F32)
-        attended_ref[:, cols[q]] = own.astype(BF16)
+        own = inner_sum(q, inner[q]) + res_ref[:, :, cols[q]].astype(F32).reshape(16, width)
+        attended_ref[:, :, cols[q]] = own.reshape(8, 2, width).astype(BF16)
         squares.append(jnp.sum(own * own, axis=1, keepdims=True))
         value = (own * gain_ref[:, cols[q]]).astype(BF16)
         normed[q] = value
@@ -426,7 +426,7 @@
         inner_back[q].start()
 
     def close_back(q):
-        out_ref[:, cols[q]] = inner_sum(q, inner_back[q]).astype(BF16)
+        out_ref[:, :, cols[q]] = inner_sum(q, inner_back[q]).reshape(8, 2, width).astype(BF16)
 
     waves(
         FLOWS // 2,
@@ -448,7 +448,7 @@
 
 PIECE = 16
 VMEM_LIMIT = 66 * 1024 * 1000
-SENDS = 2
+SENDS = 4
 
 
 def attend_kernel(
@@ -503,8 +503,6 @@
     across = (((1,), (1,)), ((), ()))
 
     def attend(r):
-        for load in loads[r]:
-            load.wait()
         old = jnp.dot(q[r], kt[r], preferred_element_type=F32) * score_scale
         old = jnp.where(position < len_ref[r], old, -jnp.inf)
         new = lax.dot_general(q[r], fresh_ref[r], across, preferred_element_type=F32) * score_scale
@@ -526,6 +524,8 @@
     per_send = pairs // SENDS
     copies = {}
     for p in range(pairs):
+        for load in loads[2 * p] + loads[2 * p + 1]:
+            load.wait()
         both = jnp.concatenate([attend(2 * p), attend(2 * p + 1)], axis=0)
         piece = jnp.dot(order, both, preferred_element_type=F32).astype(BF16)
         sent[:, p] = piece.reshape(RING * RING, PIECE, rank)
@@ -616,14 +616,14 @@
     depth, model_width = output_weight.shape
     width = model_width // FLOWS
     half = down.shape[0]
-    tokens, slots = v.shape[0], 4 * residual.shape[0]
+    tokens, slots = v.shape[0], 8 * residual.shape[0]
     copies = (12 + 7 + 1 + 9) * FLOWS + 15 + 7
     return pl.pallas_call(
         layer_kernel,
         name="layer",
         out_shape=(
-            jax.ShapeDtypeStruct((tokens // 16, model_width), BF16),
-            jax.ShapeDtypeStruct((tokens // 16, model_width), BF16),
+            jax.ShapeDtypeStruct(residual.shape, BF16),
+            jax.ShapeDtypeStruct(residual.shape, BF16),
         ),
         in_specs=vmem_specs(1) + [pl.BlockSpec(memory_space=pl.ANY)] * 4 + vmem_specs(4),
         out_specs=tuple(vmem_specs(2)),
@@ -685,12 +685,12 @@
         gate_weight[0],
         up_weight[0],
         down_weight[0],
-        residual.reshape(req_dev * steps_here, model_width),
+        residual,
         norm_gain.reshape(1, model_width),
         router.T,
         jnp.transpose(expert_ids, (1, 2, 0)).reshape(-1, expert_ids.shape[0]),
     )
-    return (attended.reshape(residual.shape), summed.reshape(residual.shape))
+    return (attended, summed)
 
 
 def solution(mesh):

time: 168 us -> 164 us (0.976)
  Pallas kernels: 162 us -> 159 us
    reshape x3 -> x0, local copies, waits for them, and re-layouts: 5.14 us -> none  [the longest x2 3.42 us: local(): return (attended.reshape(residual.shape), summed.reshape(residual.shape))]
    unnamed x0 -> x2, local copies, waits for them, and re-layouts: none -> 3.57 us
    pallas_call x1, Pallas kernels: 32.8 us -> 30.7 us  [attend(): pl.pallas_call(attend_kernel, name='attend', out_shape=jax.ShapeDtypeStru...]
where the time goes in v2:
time: 164 us; the launch traced here: 163 us
  Pallas kernels  159 us (97%)
  local copies, waits for them, and re-layouts  3.57 us (2%)
    pallas_call x1, Pallas kernels, layer(): pl.pallas_call(layer_kernel, name='layer', out_shape=(jax.ShapeDtypeStruc...  128 us
    pallas_call x1, Pallas kernels, attend(): pl.pallas_call(attend_kernel, name='attend', out_shape=jax.ShapeDtypeStru...  30.7 us
    unnamed x2, local copies, waits for them, and re-layouts  3.57 us

profile of v2, /device:TPU:0, one launch (start us, length us, event | category | flops | bytes accessed | tf_op | source)
XLA Modules:
  0.0 163.3 jit_solution(9110904187222536696)
XLA Ops:
  0.6 30.7 %attend.1 = bf16[4,64,512]{2,1,0:T(8,128)(2,1)} custom-call(s32[8]{0:T(128)} %len_ref.1, s32[1,8]{1,0:T(1,128)} %hand_ref.1, bf16[8,128,576]{2,1,0:T(8,128)(2,1)} %bitcast.15, bf16[8,576,512]{2,1,0:T(8,128)(2,1)} %bitcast.11, bf16[8,2,576]{2,1,0:T(2,128)(2,1)} %fresh_ref.1, bf16[4,512,128]{2,1,0:T(8,128)(2,1)} %w_ref.1), custom_call_target="tpu_custom_call" | custom-call | tf_op jit(solution)/shard_map/attend/pallas_call | solution.py:583
  31.3 128.4 %layer.1 = (bf16[8,2,7168]{2,1,0:T(2,128)(2,1)}, bf16[8,2,7168]{2,1,0:T(2,128)(2,1)}) custom-call(bf16[256,512]{1,0:T(8,128)(2,1)} %bitcast.16, bf16[512,7168]{1,0:T(8,128)(2,1)} %wo_hbm.1, bf16[7168,256]{1,0:T(8,128)(2,1)} %bitcast.12, bf16[7168,256]{1,0:T(8,128)(2,1)} %bitcast.13, bf16[256,7168]{1,0:T(8,128)(2,1)} %bitcast.14, ...), custom_call_target="tpu_custom_call" | custom-call | tf_op jit(solution)/shard_map/layer/pallas_call | solution.py:621
  159.8 1.8 %copy.18 = bf16[8,2,7168]{2,1,0:T(2,128)(2,1)} copy(bf16[8,2,7168]{2,1,0:T(2,128)(2,1)} %get-tuple-element.4) | data formatting | bytes 458752
  161.6 1.8 %copy.19 = bf16[8,2,7168]{2,1,0:T(2,128)(2,1)} copy(bf16[8,2,7168]{2,1,0:T(2,128)(2,1)} %get-tuple-element.5) | data formatting | bytes 458752
